TPU v7x, 256 devices: a whole 4x4x8 slice. The times are simulated.
256 devices in a mesh: space: 64 (over x, z, core), chan: 4 (over y).
Axes of the slice: x: 4, y: 4, z: 8, core: 2. Of those that a mesh axis runs over, the one named last changes fastest.
Arguments:
- features: bfloat16 [8192, 512], P('space', 'chan'), may hold values from -6 to 6
- mask: int32 [8192], P('space'), may hold values 0 or 1
- rulebook: int32 [128, 27], P('space'), may hold values from -1 to 127, as said below
- weight_first: bfloat16 [512, 27, 512], P('space', None, 'chan'), may hold values from -0.0546875 to 0.0546875
- weight_second: bfloat16 [512, 27, 512], P('space', None, 'chan'), may hold values from -0.0546875 to 0.0546875
- cotangent: bfloat16 [8192, 512], P('space', 'chan'), may hold values from -6 to 6
Outputs:
- output: bfloat16 [8192, 512], P('space', 'chan')
- features_grad: bfloat16 [8192, 512], P('space', 'chan')
- weight_first_grad: float32 [512, 27, 512], P('space', None, 'chan')
- weight_second_grad: float32 [512, 27, 512], P('space', None, 'chan')
Inputs may be any that keep to these rules, and one draw needn't show every extreme that they name: `rulebook`: entry [b, c] is the brick that feeds brick b through brick offset c, or -1 for none; entry 13 is b itself. A brick of another device belongs to a device s one or two indices away; if it feeds the device s + 1, s + 2, s - 1 or s - 2 (k = 0, 1, 2, 3 respectively), it is brick s * 2 + ((k + h) mod 2) for some h below 1.
All inputs are finite; a program needn't handle non-finite values. No bound on the sum of `mask` on one device may be relied on, other than what follows from the above.
Results may differ from a plain program's by a relative error of at most 0.005.
Values may be sent and summed in bfloat16 or wider, within the bound.
No kernel may reach another device: no remote copies, remote signals or barrier semaphores. Data moves between devices by JAX's collectives and lax.ppermute only.
A program may use at most 128 MiB of HBM per device.

v0:
```python
import jax
import jax.numpy as jnp
import numpy as np
from jax import lax
from jax.sharding import PartitionSpec as P

HB = 1
direction_steps = (1, 2, -1, -2)


def passed_along(value, axis, by):
    devices = lax.axis_size(axis)
    pairs = [(i, i + by) for i in range(devices) if 0 <= i + by < devices]
    return lax.ppermute(value, axis, pairs)


def offset_tables():
    brick_table = np.zeros((27, 64), np.int32)
    cell_table = np.zeros((27, 64), np.int32)
    for offset in range(27):
        moves = (offset // 9 - 1, offset // 3 % 3 - 1, offset % 3 - 1)
        for voxel in range(64):
            cells = (voxel // 16, voxel // 4 % 4, voxel % 4)
            target = [cells[axis_number] + moves[axis_number] for axis_number in range(3)]
            brick_table[offset, voxel] = (
                (target[0] // 4 + 1) * 9 + (target[1] // 4 + 1) * 3 + (target[2] // 4 + 1)
            )
            cell_table[offset, voxel] = target[0] % 4 * 16 + target[1] % 4 * 4 + target[2] % 4
    return (brick_table, cell_table)


def on_device(features, mask, rulebook, weight_first, weight_second, cotangent):
    brick_table, cell_table = offset_tables()
    bricks = rulebook.shape[0]
    spread = HB
    row_count = features.shape[0]
    halo_rows = 4 * spread * 64
    device_index = lax.axis_index("space")
    owner_device = rulebook // bricks
    within = rulebook % bricks
    sources = device_index - jnp.array(direction_steps, jnp.int32)
    lent_table = (
        jnp.arange(4, dtype=jnp.int32)[:, None] * spread
        + jnp.arange(spread, dtype=jnp.int32)[None, :]
    ) % bricks
    matches = (owner_device[:, :, None, None] == sources[None, None, :, None]) & (
        within[:, :, None, None] == lent_table[None, None]
    )
    numbers = bricks + jnp.arange(4 * spread, dtype=jnp.int32).reshape(4, spread)
    remote = jnp.sum(jnp.where(matches, numbers, 0), axis=(2, 3))
    slot_index = jnp.where(
        rulebook < 0, bricks + 4 * spread, jnp.where(owner_device == device_index, within, remote)
    )
    lookup = slot_index[:, brick_table] * 64 + cell_table[None]
    lookup = jnp.transpose(lookup, (1, 0, 2)).reshape(27, row_count).astype(jnp.int32)
    active = mask.astype(jnp.float32)[:, None]
    masked = (features.astype(jnp.float32) * active).astype(jnp.bfloat16)

    def outgoing(source, position):
        shaped = source.reshape(bricks, 64, source.shape[1])
        return jnp.take(shaped, lent_table[position], axis=0).reshape(spread * 64, source.shape[1])

    def extend(source):
        gathered = lax.all_gather(source, "chan", axis=1, tiled=True)
        blocks = [gathered]
        for position, offset in enumerate(direction_steps):
            blocks.append(passed_along(outgoing(gathered, position), "space", offset))
        blocks.append(jnp.zeros((64, gathered.shape[1]), jnp.bfloat16))
        return jnp.concatenate(blocks, 0)

    def lend_back(own_rows, returned, position):
        shaped = own_rows.reshape(bricks, 64, own_rows.shape[1])
        shaped = shaped.at[lent_table[position]].add(
            returned.reshape(spread, 64, own_rows.shape[1])
        )
        return shaped.reshape(row_count, own_rows.shape[1])

    def settle(running):
        summed = lax.psum_scatter(
            running[: row_count + halo_rows], "chan", scatter_dimension=1, tiled=True
        )
        own_rows = summed[:row_count]
        for position, offset in enumerate(direction_steps):
            block_start = row_count + position * spread * 64
            returned = passed_along(
                summed[block_start : block_start + spread * 64], "space", -offset
            )
            own_rows = lend_back(own_rows, returned, position)
        return own_rows

    def weight_term(extended, gradient):

        def advance(offset):
            picked = jnp.take(extended, lookup[offset], axis=0)
            return lax.dot_general(
                picked, gradient, (((0,), (0,)), ((), ())), preferred_element_type=jnp.float32
            )

        stacked = lax.map(advance, jnp.arange(27, dtype=jnp.int32))
        return jnp.transpose(stacked, (1, 0, 2))

    ext_in = extend(masked)
    table_rows = ext_in.shape[0]
    width = ext_in.shape[1]
    initial = jnp.zeros((row_count, weight_first.shape[2]), jnp.float32)
    segment = lax.all_gather(weight_first, "space", axis=0, tiled=True)
    columns = ext_in

    def advance(offset, running):
        picked = jnp.take(columns, lookup[offset], axis=0)
        kernel = lax.dynamic_index_in_dim(segment, offset, 1, keepdims=False)
        return running + jnp.dot(picked, kernel, preferred_element_type=jnp.float32)

    first_act = active * lax.fori_loop(0, 27, advance, initial)
    hidden = jax.nn.silu(first_act).astype(jnp.bfloat16)
    ext_hidden = extend(hidden)
    second_whole = lax.all_gather(weight_second, "space", axis=0, tiled=True)

    def forward_step(offset, running):
        picked = jnp.take(ext_hidden, lookup[offset], axis=0)
        kernel = lax.dynamic_index_in_dim(second_whole, offset, 1, keepdims=False)
        return running + jnp.dot(picked, kernel, preferred_element_type=jnp.float32)

    second_act = active * lax.fori_loop(
        0, 27, forward_step, jnp.zeros((row_count, second_whole.shape[2]), jnp.float32)
    )
    output = second_act.astype(jnp.bfloat16)
    grad_second = (cotangent.astype(jnp.float32) * active).astype(jnp.bfloat16)
    weight_second_grad = lax.psum_scatter(
        weight_term(ext_hidden, grad_second), "space", scatter_dimension=0, tiled=True
    )

    def backward_step(offset, running):
        kernel = lax.dynamic_index_in_dim(second_whole, offset, 1, keepdims=False)
        contrib = lax.dot_general(
            grad_second, kernel, (((1,), (1,)), ((), ())), preferred_element_type=jnp.float32
        )
        return running.at[lookup[offset]].add(contrib)

    hidden_grad = settle(
        lax.fori_loop(0, 27, backward_step, jnp.zeros((table_rows, width), jnp.float32))
    )
    sigmoid_first = jax.nn.sigmoid(first_act)
    grad_first = (
        active * hidden_grad * sigmoid_first * (1.0 + first_act * (1.0 - sigmoid_first))
    ).astype(jnp.bfloat16)
    weight_first_grad = lax.psum_scatter(
        weight_term(ext_in, grad_first), "space", scatter_dimension=0, tiled=True
    )

    def add_back(running, segment):
        columns = running

        def advance(offset, current):
            kernel = lax.dynamic_index_in_dim(segment, offset, 1, keepdims=False)
            contrib = lax.dot_general(
                grad_first, kernel, (((1,), (1,)), ((), ())), preferred_element_type=jnp.float32
            )
            return current.at[lookup[offset]].add(contrib)

        columns = lax.fori_loop(0, 27, advance, columns)
        return columns

    running = add_back(
        jnp.zeros((table_rows, width), jnp.float32),
        lax.all_gather(weight_first, "space", axis=0, tiled=True),
    )
    features_grad = (active * settle(running)).astype(jnp.bfloat16)
    return (output, features_grad, weight_first_grad, weight_second_grad)


def solution(mesh):
    placed = (
        P("space", "chan"),
        P("space"),
        P("space", None),
        P("space", None, "chan"),
        P("space", None, "chan"),
        P("space", "chan"),
    )
    return jax.shard_map(
        on_device,
        mesh=mesh,
        in_specs=placed,
        out_specs=(
            P("space", "chan"),
            P("space", "chan"),
            P("space", None, "chan"),
            P("space", None, "chan"),
        ),
        check_vma=False,
    )
```

profile of v0, /device:TPU:8, one launch (start us, length us, event | category | flops | bytes accessed | tf_op | source)
XLA Modules:
  0.0 875.7 jit_solution(18097774328851206864)
XLA Ops:
  10.5 3.3 gather_fusion.4
  16.8 71.8 %all-gather.5.cloned.1.call-done = bf16[512,27,128]{2,0,1:T(8,128)(2,1)} async-done(((bf16[8,27,128]{2,0,1:T(8,128)(2,1)}), bf16[512,27,128]{2,0,1:T(8,128)(2,1)}) %all-gather.5.cloned.1.call-update) | async-done | bytes 3538960 | tf_op jit(solution)/shard_map/all_gather | solution.py:117
  88.7 80.3 %while.83 = (s32[]{:T(128)}, f32[448,512]{1,0:T(8,128)S(1)}, s32[27,128]{1,0:T(8,128)S(1)}, bf16[512,27,128]{2,0,1:T(8,128)(2,1)}, bf16[128,128]{1,0:T(8,128)(2,1)S(1)}, /*index=5*/s32[]{:T(128)}) while((s32[]{:T(128)}, f32[448,512]{1,0:T(8,128)S(1)}, s32[27,128]{1,0:T(8,128)S(1)}, bf16[512,27,128]{2,0,1:T(8,128)(2,1)}, ...), condition=%wide.region_7.10_spmd, body=%wide.region_5.9_spmd.sunk | while | flops 16843136 | bytes 1738325 | solution.py:141
  90.0 1.7 scatter_fusion
  96.0 1.7 scatter_fusion
  101.9 1.7 scatter_fusion
  104.9 1.7 scatter_fusion
  110.8 1.7 scatter_fusion
  116.8 1.7 scatter_fusion
  119.7 1.7 scatter_fusion
  122.7 1.7 scatter_fusion
  125.7 1.7 scatter_fusion
  131.6 1.7 scatter_fusion
  137.6 1.7 scatter_fusion
  179.1 11.7 %all_gather.13 = bf16[128,512]{1,0:T(8,128)(2,1)S(1)} all-gather(bf16[128,128]{1,0:T(8,128)(2,1)S(1)} %get-tuple-element.700), channel_id=1, replica_groups=mesh['space'=64,'chan'=4] {'chan'}, dimensions={1}, use_global_device_ids=true | all-gather | bytes 163840 | tf_op jit(solution)/shard_map/all_gather | solution.py:64
  192.1 4.1 collective-permute-start.1
  199.8 5.2 collective-permute-done.3
  207.2 65.6 %all-gather.3.cloned.1.call-done = bf16[512,27,128]{2,0,1:T(8,128)(2,1)} async-done(((bf16[8,27,128]{2,0,1:T(8,128)(2,1)}), bf16[512,27,128]{2,0,1:T(8,128)(2,1)}) %all-gather.3.cloned.1.call-update) | async-done | bytes 3538960 | tf_op jit(solution)/shard_map/all_gather | solution.py:106
  272.7 55.7 %while.87 = (s32[]{:T(128)}, f32[128,128]{1,0:T(8,128)S(1)}, s32[27,128]{1,0:T(8,128)S(1)}, bf16[448,512]{1,0:T(8,128)(2,1)S(1)}, bf16[512,27,128]{2,0,1:T(8,128)(2,1)}, /*index=5*/s32[]{:T(128)}, s32[]{:T(128)}) while((s32[]{:T(128)}, f32[128,128]{1,0:T(8,128)S(1)}, s32[27,128]{1,0:T(8,128)S(1)}, bf16[448,512]{1,0:T(8,128)(2,1)S(1)}, ...), condition=%wide.region_2.5_spmd.clone, body=%wide.region_1.4_spmd.clone.sunk | while | flops 16877316 | bytes 661863 | solution.py:114
  329.8 2.2 collective-permute-start.10
  332.0 4.3 collective-permute-start.11
  339.1 80.3 %while.84 = (s32[]{:T(128)}, f32[448,512]{1,0:T(8,128)S(1)}, s32[27,128]{1,0:T(8,128)S(1)}, bf16[512,27,128]{2,0,1:T(8,128)(2,1)}, bf16[128,128]{1,0:T(8,128)(2,1)S(1)}, /*index=5*/s32[]{:T(128)}) while((s32[]{:T(128)}, f32[448,512]{1,0:T(8,128)S(1)}, s32[27,128]{1,0:T(8,128)S(1)}, bf16[512,27,128]{2,0,1:T(8,128)(2,1)}, ...), condition=%wide.region_15.18_spmd, body=%wide.region_13.17_spmd.sunk | while | flops 16843136 | bytes 1738325 | solution.py:161
  420.4 11.2 %all_gather.15 = bf16[128,512]{1,0:T(8,128)(2,1)S(1)} all-gather(bf16[128,128]{1,0:T(8,128)(2,1)S(1)} %get-tuple-element.688), channel_id=1, replica_groups=mesh['space'=64,'chan'=4] {'chan'}, dimensions={1}, use_global_device_ids=true | all-gather | bytes 163840 | tf_op jit(solution)/shard_map/all_gather | solution.py:64
  433.0 4.3 collective-permute-start.5
  439.9 3.7 broadcast.332.clone
  443.6 119.1 %while.85 = (s32[]{:T(128)}, f32[27,512,128]{2,1,0:T(8,128)}, s32[27]{0:T(128)S(1)}, s32[27,128]{1,0:T(8,128)S(1)}, bf16[448,512]{1,0:T(8,128)(2,1)S(1)}, /*inde...) while((s32[]{:T(128)}, f32[27,512,128]{2,1,0:T(8,128)}, s32[27]{0:T(128)S(1)}, ...), condition=%wide.region_18.21_spmd, body=%wide.region_17.20_spmd.sunk | while | flops 16844548 | bytes 694683 | solution.py:99
  563.0 3.7 broadcast.332.clone.1
  566.6 119.1 %while.86 = (s32[]{:T(128)}, f32[27,512,128]{2,1,0:T(8,128)}, s32[27]{0:T(128)S(1)}, s32[27,128]{1,0:T(8,128)S(1)}, bf16[448,512]{1,0:T(8,128)(2,1)S(1)}, /*inde...) while((s32[]{:T(128)}, f32[27,512,128]{2,1,0:T(8,128)}, s32[27]{0:T(128)S(1)}, ...), condition=%wide.region_21.24_spmd, body=%wide.region_20.23_spmd.sunk | while | flops 16844548 | bytes 694683 | solution.py:99
  687.9 55.8 %while.88 = (s32[]{:T(128)}, f32[128,128]{1,0:T(8,128)S(1)}, s32[27,128]{1,0:T(8,128)S(1)}, bf16[448,512]{1,0:T(8,128)(2,1)S(1)}, bf16[512,27,128]{2,0,1:T(8,128)(2,1)}, /*index=5*/s32[]{:T(128)}, s32[]{:T(128)}) while((s32[]{:T(128)}, f32[128,128]{1,0:T(8,128)S(1)}, s32[27,128]{1,0:T(8,128)S(1)}, bf16[448,512]{1,0:T(8,128)(2,1)S(1)}, ...), condition=%wide.region_4.7_spmd.clone, body=%wide.region_3.6_spmd.clone.sunk | while | flops 16877316 | bytes 661863 | solution.py:124
  745.1 4.5 collective-permute-start.14
  749.6 5.3 collective-permute-start.15
  758.3 110.5 %reduce-scatter.11.cloned.1.call-done = f32[8,27,128]{2,0,1:T(8,128)} async-done(((f32[512,27,128]{2,0,1:T(8,128)}), f32[8,27,128]{2,0,1:T(8,128)}) %reduce-scatter.11.cloned.1.call-update) | async-done | bytes 110608 | tf_op jit(solution)/shard_map/reduce_scatter | solution.py:129
  (790 shorter events, 412.4 us)
Async XLA Ops:
  7.2 81.5 %all-gather.5.cloned.1.call-start = ((), (), s32[]{:S(2)}) async-start(), calls=%async_computation.5 | async-start | bytes 3594240 | tf_op jit(solution)/shard_map/all_gather | solution.py:117
  7.9 197.1 %reduce-scatter.5.cloned.1.call-start = ((), (), s32[]{:S(2)}) async-start(), calls=%async_computation.6 | async-start | bytes 983040 | tf_op jit(solution)/shard_map/reduce_scatter | solution.py:79
  88.7 110.1 %copy-start = (s32[3]{0:T(128)S(1)}, s32[3]{0:T(128)}, u32[]{:S(2)}) copy-start(s32[3]{0:T(128)} %constant.387.clone.1) | copy-start | bytes 40
  170.0 102.8 %all-gather.3.cloned.1.call-start = ((), (), s32[]{:S(2)}) async-start(), calls=%async_computation.4 | async-start | bytes 3594240 | tf_op jit(solution)/shard_map/all_gather | solution.py:106
  170.7 515.1 %reduce-scatter.7.cloned.1.call-start = ((), (), s32[]{:S(2)}) async-start(), calls=%async_computation.7 | async-start | bytes 983040 | tf_op jit(solution)/shard_map/reduce_scatter | solution.py:79
  190.8 8.9 %collective-permute-start = (bf16[64,512]{1,0:T(8,128)(2,1)S(1)}, bf16[64,512]{1,0:T(8,128)(2,1)S(1)}, u32[]{:S(2)}, u32[]{:S(2)}) collective-permute-start(bf16[64,512]{1,0:T(8,128)(2,1)S(1)} %get-tuple-element.686), channel_id=1, source_target_pairs={{0,4},{4,8},{8,12},{12,16},{16,20},{20,24},{24,28},{28,32},{32,36}... | collective-permute-start | bytes 196616 | tf_op jit(solution)/shard_map/ppermute | solution.py:14
  192.1 7.6 collective-permute-start.1
  196.2 3.6 collective-permute-start.2
  197.5 7.4 collective-permute-start.3
  205.0 131.3 %slice-start.1 = ((f32[384,128]{1,0:T(8,128)}), f32[128,128]{1,0:T(8,128)S(1)}, s32[]{:S(2)}) async-start(f32[384,128]{1,0:T(8,128)} %reduce-scatter.5.cloned.1.call-done), calls=%async_computation.11 | async-start | bytes 131072 | tf_op jit(solution)/shard_map/slice | solution.py:82
  205.9 130.4 %collective-permute-start.8 = (f32[64,128]{1,0:T(8,128)S(1)}, f32[64,128]{1,0:T(8,128)S(1)}, u32[]{:S(2)}, u32[]{:S(2)}) collective-permute-start(f32[64,128]{1,0:T(8,128)S(1)} %get-tuple-element.678), channel_id=1, source_target_pairs={{4,0},{8,4},{12,8},{16,12},{20,16},{24,20},{28,24},{32,28},{36,32}... | collective-permute-start | bytes 98312 | tf_op jit(solution)/shard_map/ppermute | solution.py:14
  328.5 8.5 collective-permute-start.9
  329.8 7.8 collective-permute-start.10
  332.0 6.4 collective-permute-start.11
  420.4 337.9 %reduce-scatter.9.cloned.1.call-start = ((), (), s32[]{:S(2)}) async-start(), calls=%async_computation.8 | async-start | bytes 7188480 | tf_op jit(solution)/shard_map/reduce_scatter | solution.py:147
  431.7 131.1 %collective-permute-start.4 = (bf16[64,512]{1,0:T(8,128)(2,1)S(1)}, bf16[64,512]{1,0:T(8,128)(2,1)S(1)}, u32[]{:S(2)}, u32[]{:S(2)}) collective-permute-start(bf16[64,512]{1,0:T(8,128)(2,1)S(1)} %get-tuple-element.682), channel_id=1, source_target_pairs={{0,4},{4,8},{8,12},{12,16},{16,20},{20,24},{24,28},{28,32},{32,36}... | collective-permute-start | bytes 196616 | tf_op jit(solution)/shard_map/ppermute | solution.py:14
  433.0 129.8 %collective-permute-start.5 = (bf16[64,512]{1,0:T(8,128)(2,1)S(1)}, bf16[64,512]{1,0:T(8,128)(2,1)S(1)}, u32[]{:S(2)}, u32[]{:S(2)}) collective-permute-start(bf16[64,512]{1,0:T(8,128)(2,1)S(1)} %get-tuple-element.681), channel_id=1, source_target_pairs={{0,8},{4,12},{8,16},{12,20},{16,24},{20,28},{24,32},{28,36},{32,40... | collective-permute-start | bytes 196616 | tf_op jit(solution)/shard_map/ppermute | solution.py:14
  437.3 125.6 %collective-permute-start.6 = (bf16[64,512]{1,0:T(8,128)(2,1)S(1)}, bf16[64,512]{1,0:T(8,128)(2,1)S(1)}, u32[]{:S(2)}, u32[]{:S(2)}) collective-permute-start(bf16[64,512]{1,0:T(8,128)(2,1)S(1)} %get-tuple-element.680), channel_id=1, source_target_pairs={{4,0},{8,4},{12,8},{16,12},{20,16},{24,20},{28,24},{32,28},{36,32}... | collective-permute-start | bytes 196616 | tf_op jit(solution)/shard_map/ppermute | solution.py:14
  438.6 124.3 %collective-permute-start.7 = (bf16[64,512]{1,0:T(8,128)(2,1)S(1)}, bf16[64,512]{1,0:T(8,128)(2,1)S(1)}, u32[]{:S(2)}, u32[]{:S(2)}) collective-permute-start(bf16[64,512]{1,0:T(8,128)(2,1)S(1)} %get-tuple-element.679), channel_id=1, source_target_pairs={{8,0},{12,4},{16,8},{20,12},{24,16},{28,20},{32,24},{36,28},{40,32... | collective-permute-start | bytes 196616 | tf_op jit(solution)/shard_map/ppermute | solution.py:14
  562.8 306.1 %reduce-scatter.11.cloned.1.call-start = ((), (), s32[]{:S(2)}) async-start(), calls=%async_computation.9 | async-start | bytes 7188480 | tf_op jit(solution)/shard_map/reduce_scatter | solution.py:129
  685.8 69.2 %slice-start = ((f32[384,128]{1,0:T(8,128)}), f32[128,128]{1,0:T(8,128)S(1)}, s32[]{:S(2)}) async-start(f32[384,128]{1,0:T(8,128)} %reduce-scatter.7.cloned.1.call-done), calls=%async_computation.10 | async-start | bytes 131072 | tf_op jit(solution)/shard_map/slice | solution.py:82
  686.6 68.3 %collective-permute-start.12 = (f32[64,128]{1,0:T(8,128)S(1)}, f32[64,128]{1,0:T(8,128)S(1)}, u32[]{:S(2)}, u32[]{:S(2)}) collective-permute-start(f32[64,128]{1,0:T(8,128)S(1)} %get-tuple-element.674), channel_id=1, source_target_pairs={{4,0},{8,4},{12,8},{16,12},{20,16},{24,20},{28,24},{32,28},{36,32}... | collective-permute-start | bytes 98312 | tf_op jit(solution)/shard_map/ppermute | solution.py:14
  743.8 11.8 %collective-permute-start.13 = (f32[64,128]{1,0:T(8,128)S(1)}, f32[64,128]{1,0:T(8,128)S(1)}, u32[]{:S(2)}, u32[]{:S(2)}) collective-permute-start(f32[64,128]{1,0:T(8,128)S(1)} %get-tuple-element.673), channel_id=1, source_target_pairs={{8,0},{12,4},{16,8},{20,12},{24,16},{28,20},{32,24},{36,28},{40,32... | collective-permute-start | bytes 98312 | tf_op jit(solution)/shard_map/ppermute | solution.py:14
  745.1 11.2 %collective-permute-start.14 = (f32[64,128]{1,0:T(8,128)S(1)}, f32[64,128]{1,0:T(8,128)S(1)}, u32[]{:S(2)}, u32[]{:S(2)}) collective-permute-start(f32[64,128]{1,0:T(8,128)S(1)} %get-tuple-element.672), channel_id=1, source_target_pairs={{0,4},{4,8},{8,12},{12,16},{16,20},{20,24},{24,28},{28,32},{32,36}... | collective-permute-start | bytes 98312 | tf_op jit(solution)/shard_map/ppermute | solution.py:14
  749.6 7.4 collective-permute-start.15
Sparse Core Ops, SparseCore 0:
  10.6 78.0 all-gather.4
  170.1 23.1 reduce-scatter.4
  195.9 76.8 all-gather.2
  420.5 24.8 reduce-scatter.6
  562.9 154.1 reduce-scatter.8
  721.8 146.9 reduce-scatter.10
where the time goes:
time: 880 us; the launch traced here: 876 us
  waiting for transfers between devices  255 us (29%)
  matrix products  175 us (20%)
  local copies, waits for them, and re-layouts  147 us (17%)
  loops' own time  111 us (13%)
  other arithmetic  106 us (12%)
  starting transfers between devices  37.9 us (4%)
  blocking collectives  22.9 us (3%)
  between operations  22.5 us (3%)
    reduce_scatter x1, waiting for transfers between devices, on_device(): lax.psum_scatter(weight_term(ext_hidden, grad_second), 'space', scatter_d...  111 us
    another operation x2, loops' own time, weight_term(): stacked = lax.map(advance, jnp.arange(27, dtype=jnp.int32))  106 us
    all_gather x1, waiting for transfers between devices, on_device(): second_whole = lax.all_gather(weight_second, 'space', axis=0, tiled=True)  71.8 us
    all_gather x1, waiting for transfers between devices, on_device(): segment = lax.all_gather(weight_first, 'space', axis=0, tiled=True)  65.6 us
    dot_general x54, matrix products, advance(): lax.dot_general(picked, gradient, (((0,), (0,)), ((), ())), preferred_ele...  53.9 us
    scatter-add x27, other arithmetic, backward_step(): return running.at[lookup[offset]].add(contrib)  45.9 us
    scatter-add x27, other arithmetic, advance(): return current.at[lookup[offset]].add(contrib)  45.9 us
    gather x54, local copies, waits for them, and re-layouts, advance(): picked = jnp.take(extended, lookup[offset], axis=0)  45.8 us
  transfers between devices with their start and end apart: 22, of which 5 were waited for; matrix products, arithmetic and copies ran while one was open for 30% of the time, Pallas kernels for 0%

commit v1 on v0

--- a/solution.py
+++ b/solution.py
@@ -61,7 +61,26 @@
         return jnp.take(shaped, lent_table[position], axis=0).reshape(spread * 64, source.shape[1])
 
     def extend(source):
-        gathered = lax.all_gather(source, "chan", axis=1, tiled=True)
+        devices_2, index, rows = (lax.axis_size("chan"), lax.axis_index("chan"), source.shape[1])
+        ahead = [(i_2, (i_2 + 1) % devices_2) for i_2 in range(devices_2)]
+        left = [(i_2, (i_2 - 1) % devices_2) for i_2 in range(devices_2)]
+        whole = jnp.zeros(
+            (*source.shape[:1], devices_2 * rows, *source.shape[1 + 1 :]), source.dtype
+        )
+        whole = lax.dynamic_update_slice_in_dim(whole, source, index * rows, axis=1)
+        from_left = from_right = source
+        half = devices_2 // 2
+        for step in range(1, half + 1):
+            from_left = lax.ppermute(from_left, "chan", ahead)
+            whole = lax.dynamic_update_slice_in_dim(
+                whole, from_left, (index - step) % devices_2 * rows, axis=1
+            )
+            if step < devices_2 - half:
+                from_right = lax.ppermute(from_right, "chan", left)
+                whole = lax.dynamic_update_slice_in_dim(
+                    whole, from_right, (index + step) % devices_2 * rows, axis=1
+                )
+        gathered = whole
         blocks = [gathered]
         for position, offset in enumerate(direction_steps):
             blocks.append(passed_along(outgoing(gathered, position), "space", offset))

time: 880 us -> 783 us (0.89)
  waiting for transfers between devices: 255 us -> 172 us
  blocking collectives: 22.9 us -> 0 us
    reduce_scatter x1, waiting for transfers between devices: 111 us -> 0.01 us  [on_device(): lax.psum_scatter(weight_term(ext_hidden, grad_second), 'space', scatter_d...]
    reduce_scatter x1, waiting for transfers between devices: 0.01 us -> 110 us  [on_device(): lax.psum_scatter(weight_term(ext_in, grad_first), 'space', scatter_dimens...]
    all_gather x1, waiting for transfers between devices: 65.6 us -> 0.02 us  [on_device(): segment = lax.all_gather(weight_first, 'space', axis=0, tiled=True)]
    all_gather x1, waiting for transfers between devices: 71.8 us -> 40.8 us  [on_device(): second_whole = lax.all_gather(weight_second, 'space', axis=0, tiled=True)]
    all_gather x2 -> x0, blocking collectives: 22.9 us -> none  [extend(): gathered = lax.all_gather(source, 'chan', axis=1, tiled=True)]
  transfers between devices with their start and end apart: 22 -> 28, of which waited for: 5 -> 10; matrix products, arithmetic and copies ran while one was open for 30% -> 45% of each run, Pallas kernels for 0% -> 0%
where the time goes in v1:
time: 783 us; the launch traced here: 778 us
  matrix products  175 us (22%)
  waiting for transfers between devices  172 us (22%)
  local copies, waits for them, and re-layouts  148 us (19%)
  loops' own time  111 us (14%)
  other arithmetic  107 us (14%)
  starting transfers between devices  43.3 us (6%)
  between operations  22.5 us (3%)
    reduce_scatter x1, waiting for transfers between devices, on_device(): lax.psum_scatter(weight_term(ext_in, grad_first), 'space', scatter_dimens...  110 us
    another operation x2, loops' own time, weight_term(): stacked = lax.map(advance, jnp.arange(27, dtype=jnp.int32))  106 us
    dot_general x54, matrix products, advance(): lax.dot_general(picked, gradient, (((0,), (0,)), ((), ())), preferred_ele...  54 us
    scatter-add x27, other arithmetic, backward_step(): return running.at[lookup[offset]].add(contrib)  45.9 us
    scatter-add x27, other arithmetic, advance(): return current.at[lookup[offset]].add(contrib)  45.9 us
    gather x54, local copies, waits for them, and re-layouts, advance(): picked = jnp.take(extended, lookup[offset], axis=0)  45.8 us
    all_gather x1, waiting for transfers between devices, on_device(): second_whole = lax.all_gather(weight_second, 'space', axis=0, tiled=True)  40.8 us
    ppermute x16, starting transfers between devices, passed_along(): return lax.ppermute(value, axis, pairs)  35.8 us
  transfers between devices with their start and end apart: 28, of which 10 were waited for; matrix products, arithmetic and copies ran while one was open for 45% of the time, Pallas kernels for 0%

profile of v1, /device:TPU:8, one launch (start us, length us, event | category | flops | bytes accessed | tf_op | source)
XLA Modules:
  0.0 778.2 jit_solution(1520997210466276488)
XLA Ops:
  14.5 3.3 gather_fusion.4
  29.9 3.7 collective-permute-done.2
  35.0 3.1 collective-permute-start.4
  40.7 1.7 collective-permute-done.5
  42.5 5.5 collective-permute-done.6
  48.0 40.8 %all-gather.5.cloned.1.call-done = bf16[512,27,128]{2,0,1:T(8,128)(2,1)} async-done(((bf16[8,27,128]{2,0,1:T(8,128)(2,1)}), bf16[512,27,128]{2,0,1:T(8,128)(2,1)}) %all-gather.5.cloned.1.call-update) | async-done | bytes 3538960 | tf_op jit(solution)/shard_map/all_gather | solution.py:136
  88.9 80.3 %while.83 = (s32[]{:T(128)}, f32[448,512]{1,0:T(8,128)S(1)}, s32[27,128]{1,0:T(8,128)S(1)}, bf16[512,27,128]{2,0,1:T(8,128)(2,1)}, bf16[128,128]{1,0:T(8,128)(2,1)S(1)}, /*index=5*/s32[]{:T(128)}) while((s32[]{:T(128)}, f32[448,512]{1,0:T(8,128)S(1)}, s32[27,128]{1,0:T(8,128)S(1)}, bf16[512,27,128]{2,0,1:T(8,128)(2,1)}, ...), condition=%wide.region_7.10_spmd, body=%wide.region_5.9_spmd.sunk | while | flops 16843136 | bytes 1738325 | solution.py:160
  90.1 1.7 scatter_fusion
  96.1 1.7 scatter_fusion
  102.0 1.7 scatter_fusion
  105.0 1.7 scatter_fusion
  108.0 1.7 scatter_fusion
  111.0 1.7 scatter_fusion
  116.9 1.7 scatter_fusion
  122.8 1.7 scatter_fusion
  125.8 1.7 scatter_fusion
  128.8 1.7 scatter_fusion
  131.8 1.7 scatter_fusion
  170.3 55.8 %while.87 = (s32[]{:T(128)}, f32[128,128]{1,0:T(8,128)S(1)}, s32[27,128]{1,0:T(8,128)S(1)}, bf16[448,512]{1,0:T(8,128)(2,1)S(1)}, bf16[512,27,128]{2,0,1:T(8,128)(2,1)}, /*index=5*/s32[]{:T(128)}, s32[]{:T(128)}) while((s32[]{:T(128)}, f32[128,128]{1,0:T(8,128)S(1)}, s32[27,128]{1,0:T(8,128)S(1)}, bf16[448,512]{1,0:T(8,128)(2,1)S(1)}, ...), condition=%wide.region_2.5_spmd.clone, body=%wide.region_1.4_spmd.clone.sunk | while | flops 16877316 | bytes 661863 | solution.py:133
  235.4 4.0 collective-permute-start.11
  243.2 5.2 collective-permute-done.13
  251.8 3.0 collective-permute-start.16
  254.8 4.4 collective-permute-start.17
  263.0 80.3 %while.84 = (s32[]{:T(128)}, f32[448,512]{1,0:T(8,128)S(1)}, s32[27,128]{1,0:T(8,128)S(1)}, bf16[512,27,128]{2,0,1:T(8,128)(2,1)}, bf16[128,128]{1,0:T(8,128)(2,1)S(1)}, /*index=5*/s32[]{:T(128)}) while((s32[]{:T(128)}, f32[448,512]{1,0:T(8,128)S(1)}, s32[27,128]{1,0:T(8,128)S(1)}, bf16[512,27,128]{2,0,1:T(8,128)(2,1)}, ...), condition=%wide.region_15.18_spmd, body=%wide.region_13.17_spmd.sunk | while | flops 16843136 | bytes 1738325 | solution.py:180
  344.3 3.7 broadcast.342.clone.1
  348.0 119.1 %while.86 = (s32[]{:T(128)}, f32[27,512,128]{2,1,0:T(8,128)}, s32[27]{0:T(128)S(1)}, s32[27,128]{1,0:T(8,128)S(1)}, bf16[448,512]{1,0:T(8,128)(2,1)S(1)}, /*inde...) while((s32[]{:T(128)}, f32[27,512,128]{2,1,0:T(8,128)}, s32[27]{0:T(128)S(1)}, ...), condition=%wide.region_21.24_spmd, body=%wide.region_20.23_spmd.sunk | while | flops 16844548 | bytes 694683 | solution.py:118
  467.2 3.7 broadcast.342.clone
  470.9 119.2 %while.85 = (s32[]{:T(128)}, f32[27,512,128]{2,1,0:T(8,128)}, s32[27]{0:T(128)S(1)}, s32[27,128]{1,0:T(8,128)S(1)}, bf16[448,512]{1,0:T(8,128)(2,1)S(1)}, /*inde...) while((s32[]{:T(128)}, f32[27,512,128]{2,1,0:T(8,128)}, s32[27]{0:T(128)S(1)}, ...), condition=%wide.region_18.21_spmd, body=%wide.region_17.20_spmd.sunk | while | flops 16844548 | bytes 694683 | solution.py:118
  592.3 55.8 %while.88 = (s32[]{:T(128)}, f32[128,128]{1,0:T(8,128)S(1)}, s32[27,128]{1,0:T(8,128)S(1)}, bf16[448,512]{1,0:T(8,128)(2,1)S(1)}, bf16[512,27,128]{2,0,1:T(8,128)(2,1)}, /*index=5*/s32[]{:T(128)}, s32[]{:T(128)}) while((s32[]{:T(128)}, f32[128,128]{1,0:T(8,128)S(1)}, s32[27,128]{1,0:T(8,128)S(1)}, bf16[448,512]{1,0:T(8,128)(2,1)S(1)}, ...), condition=%wide.region_4.7_spmd.clone, body=%wide.region_3.6_spmd.clone.sunk | while | flops 16877316 | bytes 661863 | solution.py:143
  649.5 3.9 collective-permute-start.20
  653.4 4.4 collective-permute-start.21
  661.2 110.2 %reduce-scatter.9.cloned.1.call-done = f32[8,27,128]{2,0,1:T(8,128)} async-done(((f32[512,27,128]{2,0,1:T(8,128)}), f32[8,27,128]{2,0,1:T(8,128)}) %reduce-scatter.9.cloned.1.call-update) | async-done | bytes 110608 | tf_op jit(solution)/shard_map/reduce_scatter | solution.py:166
  (809 shorter events, 425.9 us)
Async XLA Ops:
  7.2 81.6 %all-gather.5.cloned.1.call-start = ((), (), s32[]{:S(2)}) async-start(), calls=%async_computation.5 | async-start | bytes 3594240 | tf_op jit(solution)/shard_map/all_gather | solution.py:136
  7.9 162.3 %all-gather.3.cloned.1.call-start = ((), (), s32[]{:S(2)}) async-start(), calls=%async_computation.4 | async-start | bytes 3594240 | tf_op jit(solution)/shard_map/all_gather | solution.py:125
  9.5 19.0 %collective-permute-start = (bf16[128,128]{1,0:T(8,128)(2,1)S(1)}, bf16[128,128]{1,0:T(8,128)(2,1)S(1)}, u32[]{:S(2)}, u32[]{:S(2)}) collective-permute-start(bf16[128,128]{1,0:T(8,128)(2,1)S(1)} %get-tuple-element.674), channel_id=1, source_target_pairs={{0,1},{1,2},{2,3},{3,0},{4,5},{5,6},{6,7},{7,4},{8,9},{9,10},{10,1... | collective-permute-start | bytes 98312 | tf_op jit(solution)/shard_map/ppermute | solution.py:74
  11.1 18.8 %collective-permute-start.1 = (bf16[128,128]{1,0:T(8,128)(2,1)S(1)}, bf16[128,128]{1,0:T(8,128)(2,1)S(1)}, u32[]{:S(2)}, u32[]{:S(2)}) collective-permute-start(bf16[128,128]{1,0:T(8,128)(2,1)S(1)} %get-tuple-element.674), channel_id=1, source_target_pairs={{0,3},{1,0},{2,1},{3,2},{4,7},{5,4},{6,5},{7,6},{8,11},{9,8},{10,9... | collective-permute-start | bytes 98312 | tf_op jit(solution)/shard_map/ppermute | solution.py:79
  11.9 236.5 %reduce-scatter.5.cloned.1.call-start = ((), (), s32[]{:S(2)}) async-start(), calls=%async_computation.6 | async-start | bytes 983040 | tf_op jit(solution)/shard_map/reduce_scatter | solution.py:98
  28.5 5.1 collective-permute-start.2
  33.7 7.0 collective-permute-start.3
  35.0 5.7 collective-permute-start.4
  38.1 4.4 collective-permute-start.5
  39.4 8.6 %collective-permute-start.6 = (bf16[64,512]{1,0:T(8,128)(2,1)S(1)}, bf16[64,512]{1,0:T(8,128)(2,1)S(1)}, u32[]{:S(2)}, u32[]{:S(2)}) collective-permute-start(bf16[64,512]{1,0:T(8,128)(2,1)S(1)} %get-tuple-element.687), channel_id=1, source_target_pairs={{8,0},{12,4},{16,8},{20,12},{24,16},{28,20},{32,24},{36,28},{40,32... | collective-permute-start | bytes 196616 | tf_op jit(solution)/shard_map/ppermute | solution.py:14
  169.2 58.5 %copy-start = (s32[3]{0:T(128)S(1)}, s32[3]{0:T(128)}, u32[]{:S(2)}) copy-start(s32[3]{0:T(128)} %constant.425.clone.1) | copy-start | bytes 40
  170.2 420.0 %reduce-scatter.7.cloned.1.call-start = ((), (), s32[]{:S(2)}) async-start(), calls=%async_computation.7 | async-start | bytes 983040 | tf_op jit(solution)/shard_map/reduce_scatter | solution.py:98
  226.2 4.0 collective-permute-start.7
  228.6 3.9 collective-permute-start.8
  230.2 3.9 collective-permute-start.9
  234.1 7.9 %collective-permute-start.10 = (bf16[64,512]{1,0:T(8,128)(2,1)S(1)}, bf16[64,512]{1,0:T(8,128)(2,1)S(1)}, u32[]{:S(2)}, u32[]{:S(2)}) collective-permute-start(bf16[64,512]{1,0:T(8,128)(2,1)S(1)} %get-tuple-element.686), channel_id=1, source_target_pairs={{0,4},{4,8},{8,12},{12,16},{16,20},{20,24},{24,28},{28,32},{32,36}... | collective-permute-start | bytes 196616 | tf_op jit(solution)/shard_map/ppermute | solution.py:14
  235.4 6.6 collective-permute-start.11
  239.4 3.7 collective-permute-start.12
  240.7 7.6 collective-permute-start.13
  249.2 10.9 %collective-permute-start.14 = (f32[64,128]{1,0:T(8,128)S(1)}, f32[64,128]{1,0:T(8,128)S(1)}, u32[]{:S(2)}, u32[]{:S(2)}) collective-permute-start(f32[64,128]{1,0:T(8,128)S(1)} %get-tuple-element.682), channel_id=1, source_target_pairs={{4,0},{8,4},{12,8},{16,12},{20,16},{24,20},{28,24},{32,28},{36,32}... | collective-permute-start | bytes 98312 | tf_op jit(solution)/shard_map/ppermute | solution.py:14
  250.5 10.3 %collective-permute-start.15 = (f32[64,128]{1,0:T(8,128)S(1)}, f32[64,128]{1,0:T(8,128)S(1)}, u32[]{:S(2)}, u32[]{:S(2)}) collective-permute-start(f32[64,128]{1,0:T(8,128)S(1)} %get-tuple-element.681), channel_id=1, source_target_pairs={{8,0},{12,4},{16,8},{20,12},{24,16},{28,20},{32,24},{36,28},{40,32... | collective-permute-start | bytes 98312 | tf_op jit(solution)/shard_map/ppermute | solution.py:14
  251.8 9.6 %collective-permute-start.16 = (f32[64,128]{1,0:T(8,128)S(1)}, f32[64,128]{1,0:T(8,128)S(1)}, u32[]{:S(2)}, u32[]{:S(2)}) collective-permute-start(f32[64,128]{1,0:T(8,128)S(1)} %get-tuple-element.680), channel_id=1, source_target_pairs={{0,4},{4,8},{8,12},{12,16},{16,20},{20,24},{24,28},{28,32},{32,36}... | collective-permute-start | bytes 98312 | tf_op jit(solution)/shard_map/ppermute | solution.py:14
  254.8 7.3 collective-permute-start.17
  344.2 317.0 %reduce-scatter.11.cloned.1.call-start = ((), (), s32[]{:S(2)}) async-start(), calls=%async_computation.9 | async-start | bytes 7188480 | tf_op jit(solution)/shard_map/reduce_scatter | solution.py:148
  467.2 304.2 %reduce-scatter.9.cloned.1.call-start = ((), (), s32[]{:S(2)}) async-start(), calls=%async_computation.8 | async-start | bytes 7188480 | tf_op jit(solution)/shard_map/reduce_scatter | solution.py:166
  590.2 67.6 %slice-start = ((f32[384,128]{1,0:T(8,128)}), f32[128,128]{1,0:T(8,128)S(1)}, s32[]{:S(2)}) async-start(f32[384,128]{1,0:T(8,128)} %reduce-scatter.7.cloned.1.call-done), calls=%async_computation.10 | async-start | bytes 131072 | tf_op jit(solution)/shard_map/slice | solution.py:101
  591.0 66.8 %collective-permute-start.18 = (f32[64,128]{1,0:T(8,128)S(1)}, f32[64,128]{1,0:T(8,128)S(1)}, u32[]{:S(2)}, u32[]{:S(2)}) collective-permute-start(f32[64,128]{1,0:T(8,128)S(1)} %get-tuple-element.678), channel_id=1, source_target_pairs={{4,0},{8,4},{12,8},{16,12},{20,16},{24,20},{28,24},{32,28},{36,32}... | collective-permute-start | bytes 98312 | tf_op jit(solution)/shard_map/ppermute | solution.py:14
  648.2 10.3 %collective-permute-start.19 = (f32[64,128]{1,0:T(8,128)S(1)}, f32[64,128]{1,0:T(8,128)S(1)}, u32[]{:S(2)}, u32[]{:S(2)}) collective-permute-start(f32[64,128]{1,0:T(8,128)S(1)} %get-tuple-element.677), channel_id=1, source_target_pairs={{8,0},{12,4},{16,8},{20,12},{24,16},{28,20},{32,24},{36,28},{40,32... | collective-permute-start | bytes 98312 | tf_op jit(solution)/shard_map/ppermute | solution.py:14
  649.5 9.6 %collective-permute-start.20 = (f32[64,128]{1,0:T(8,128)S(1)}, f32[64,128]{1,0:T(8,128)S(1)}, u32[]{:S(2)}, u32[]{:S(2)}) collective-permute-start(f32[64,128]{1,0:T(8,128)S(1)} %get-tuple-element.676), channel_id=1, source_target_pairs={{0,4},{4,8},{8,12},{12,16},{16,20},{20,24},{24,28},{28,32},{32,36}... | collective-permute-start | bytes 98312 | tf_op jit(solution)/shard_map/ppermute | solution.py:14
  653.4 6.5 collective-permute-start.21
Sparse Core Ops, SparseCore 0:
  10.6 78.1 all-gather.4
  91.3 74.3 all-gather.2
  170.3 21.9 reduce-scatter.4
  344.4 26.3 reduce-scatter.6
  467.3 152.3 reduce-scatter.10
  624.4 146.9 reduce-scatter.8
